TPU v7x, 32 devices: a whole 2x2x4 slice. The times are simulated.
32 devices in a mesh: dap: 8 (over z, x), head: 4 (over y, core).
Axes of the slice: x: 2, y: 2, z: 4, core: 2. Of those that a mesh axis runs over, the one named last changes fastest.
Arguments:
- multiple_aligned_family: bfloat16 [128, 128, 256], P('dap')
- homolog_present_flags: int32 [128], replicated, may hold values from 0 to 1, as said below
- amino_present_flags: int32 [128], replicated, may hold values 0 or 1
- focus_layernorm_scaling: float32 [256], replicated, may hold values from 0.5 to 1.5
- focus_layernorm_offset: float32 [256], replicated, may hold values from -1.8 to 1.8
- combined_focus_matrices: bfloat16 [256, 4, 256], P(None, None, 'head')
- sigmoid_switch_offset: float32 [256], P('head'), may hold values from -4 to 4
- focus_final_matrix: bfloat16 [256, 256], P('head'), may hold values from -0.375 to 0.375
- focus_final_offset: float32 [256], replicated, may hold values from -3 to 3
- tensor_layernorm_scaling: float32 [256], replicated, may hold values from 0.5 to 1.5
- tensor_layernorm_offset: float32 [256], replicated, may hold values from -1.8 to 1.8
- tensor_product_factors: bfloat16 [256, 2, 32], replicated, may hold values from -0.375 to 0.375
- tensor_final_matrix: float32 [1024, 128], replicated, may hold values from -0.1875 to 0.1875
- tensor_final_offset: float32 [128], replicated, may hold values from -4 to 4
Outputs:
- alignment_output: bfloat16 [128, 128, 256], P(('dap', 'head'))
- pair_mean_update: float32 [128, 128, 128], P('dap', 'head')
Inputs may be any that keep to these rules, and one draw needn't show every extreme that they name: homolog_present_flags[0] is always 1.
All inputs are finite; a program needn't handle non-finite values.
Results may differ from a plain program's by a relative error of at most 0.005.
Values may be sent and summed in bfloat16 or wider, within the bound.
A program may use at most 256 MiB of HBM per device.

v0:
```python
import jax
import jax.numpy as jnp
from jax import lax
from jax.sharding import PartitionSpec as P

DH = 32
CO = 32


def layer_norm(value, gain, bias):
    mean = jnp.mean(value, -1, keepdims=True)
    centred = value - mean
    spread = jnp.mean(centred * centred, -1, keepdims=True)
    return centred * lax.rsqrt(spread + 1e-05) * gain + bias


def attend_column(query, keys, values, gate, keep):
    scores = jnp.einsum("shd,thd->hst", query, keys, preferred_element_type=jnp.float32)
    scores = jnp.where(keep[None, None, :], scores, jnp.float32(-1000000000.0))
    top = jnp.max(scores, -1, keepdims=True)
    weights = jnp.exp(scores - top)
    probs = (weights / jnp.sum(weights, -1, keepdims=True)).astype(jnp.bfloat16)
    mixed = jnp.einsum("hst,thd->shd", probs, values, preferred_element_type=jnp.float32)
    return (mixed * gate).astype(jnp.bfloat16)


def per_device(
    multiple_aligned_family,
    homolog_present_flags,
    amino_present_flags,
    focus_layernorm_scaling,
    focus_layernorm_offset,
    combined_focus_matrices,
    sigmoid_switch_offset,
    focus_final_matrix,
    focus_final_offset,
    tensor_layernorm_scaling,
    tensor_layernorm_offset,
    tensor_product_factors,
    tensor_final_matrix,
    tensor_final_offset,
):
    parallel_devices = lax.axis_size("dap")
    n_head = lax.axis_size("head")
    head_id = lax.axis_index("head")
    dap_id = lax.axis_index("dap")
    homolog_shard_number, amino_total, feature_dimension = multiple_aligned_family.shape
    total_seqs = homolog_present_flags.shape[0]
    residue_device_count = amino_total // parallel_devices
    local_heads = sigmoid_switch_offset.shape[0] // DH
    keep = homolog_present_flags > 0
    weights_in = combined_focus_matrices.reshape(feature_dimension, 4 * local_heads * DH)
    gate_shift = sigmoid_switch_offset.reshape(local_heads, DH)
    bundled_focus_units = multiple_aligned_family.reshape(
        homolog_shard_number, parallel_devices, residue_device_count, feature_dimension
    )
    received = lax.all_to_all(bundled_focus_units, "dap", split_axis=1, concat_axis=0, tiled=True)
    block = received[:, 0]
    count = block.shape[1]
    normed = layer_norm(
        block.astype(jnp.float32), focus_layernorm_scaling, focus_layernorm_offset
    ).astype(jnp.bfloat16)
    projected = jnp.dot(
        normed.reshape(total_seqs * count, feature_dimension),
        weights_in,
        preferred_element_type=jnp.float32,
    )
    projected = projected.reshape(total_seqs, count, 4, local_heads, DH)
    query = jnp.moveaxis((projected[:, :, 0] * DH ** (-0.5)).astype(jnp.bfloat16), 1, 0)
    keys = jnp.moveaxis(projected[:, :, 1].astype(jnp.bfloat16), 1, 0)
    values = jnp.moveaxis(projected[:, :, 2].astype(jnp.bfloat16), 1, 0)
    gate = jnp.moveaxis(jax.nn.sigmoid(projected[:, :, 3] + gate_shift), 1, 0)

    def single(operands):
        return attend_column(operands[0], operands[1], operands[2], operands[3], keep)

    attended = lax.map(single, (query, keys, values, gate))
    attended = jnp.moveaxis(attended, 0, 1).reshape(total_seqs * count, local_heads * DH)
    partial_value = jnp.dot(attended, focus_final_matrix, preferred_element_type=jnp.float32)
    partial_value, columns = (
        partial_value.reshape(total_seqs, 1, count, feature_dimension),
        received,
    )
    group = homolog_shard_number // n_head
    columns = columns.reshape(
        parallel_devices, n_head, group, residue_device_count, feature_dimension
    )
    partial_value = partial_value.reshape(
        parallel_devices, n_head, group, residue_device_count, feature_dimension
    )
    summed = lax.psum(partial_value.astype(jnp.bfloat16), "head").astype(jnp.float32)
    summed_mine = lax.dynamic_index_in_dim(summed, head_id, 1, keepdims=True)
    own = lax.dynamic_index_in_dim(columns, head_id, 1, keepdims=True)
    mine = (own.astype(jnp.float32) + summed_mine + focus_final_offset).astype(jnp.bfloat16)
    alignment_rows = lax.all_to_all(
        mine.reshape(parallel_devices * group, residue_device_count, feature_dimension),
        "dap",
        split_axis=0,
        concat_axis=1,
        tiled=True,
    )
    seq_keep = homolog_present_flags.astype(jnp.float32).reshape(parallel_devices, n_head, group)
    row_keep = lax.dynamic_slice_in_dim(
        amino_present_flags, dap_id * residue_device_count, residue_device_count
    ).astype(jnp.float32)
    stack = mine.reshape(parallel_devices * group, residue_device_count, feature_dimension)
    mask_seq = lax.dynamic_index_in_dim(seq_keep, head_id, 1, keepdims=False).reshape(
        parallel_devices * group
    )
    left_weight = tensor_product_factors[:, 0]
    right_weight = tensor_product_factors[:, 1]
    used = stack.shape[0]
    opm_normed = layer_norm(
        stack.astype(jnp.float32), tensor_layernorm_scaling, tensor_layernorm_offset
    ).astype(jnp.bfloat16)
    flat = opm_normed.reshape(used * residue_device_count, feature_dimension)
    keep_rs = mask_seq[:, None, None] * row_keep[None, :, None]
    left = (
        jnp.dot(flat, left_weight, preferred_element_type=jnp.float32).reshape(
            used, residue_device_count, -1
        )
        * keep_rs
    ).astype(jnp.bfloat16)
    right = (
        jnp.dot(flat, right_weight, preferred_element_type=jnp.float32).reshape(
            used, residue_device_count, CO
        )
        * keep_rs
    ).astype(jnp.bfloat16)
    piece = lax.all_gather(right, "dap", axis=1, tiled=True)
    outer = lax.dot_general(
        left, piece, (((0,), (0,)), ((), ())), preferred_element_type=jnp.float32
    )
    outer = outer.transpose(0, 2, 1, 3).reshape(residue_device_count, piece.shape[1], -1)
    partial_pair = jnp.dot(
        outer,
        tensor_final_matrix,
        precision=lax.Precision.HIGHEST,
        preferred_element_type=jnp.float32,
    )
    pair = lax.psum_scatter(partial_pair, "head", scatter_dimension=1, tiled=True)
    col_width = amino_total // n_head
    col_keep = lax.dynamic_slice_in_dim(amino_present_flags, head_id * col_width, col_width).astype(
        jnp.float32
    )
    count = jnp.sum(homolog_present_flags).astype(jnp.float32)
    norm = jnp.maximum(count * row_keep[:, None] * col_keep[None, :], 1.0)
    pair_mean_update = (pair + tensor_final_offset) / norm[:, :, None]
    return (alignment_rows, pair_mean_update)


def solution(mesh):
    return jax.shard_map(
        per_device,
        mesh=mesh,
        in_specs=(
            P("dap", None, None),
            P(),
            P(),
            P(),
            P(),
            P(None, None, "head"),
            P("head"),
            P("head", None),
            P(),
            P(),
            P(),
            P(),
            P(),
            P(),
        ),
        out_specs=(P(("dap", "head"), None, None), P("dap", "head", None)),
        check_vma=False,
    )
```

profile of v0, /device:TPU:0, one launch (start us, length us, event | category | flops | bytes accessed | tf_op | source)
XLA Modules:
  0.0 189.5 jit_solution(11915135432507252343)
XLA Ops:
  7.2 2.4 %copy.23 = bf16[16,8,16,256]{3,2,0,1:T(8,128)(2,1)} copy(bf16[16,8,16,256]{3,2,1,0:T(8,128)(2,1)} %bitcast.152) | data formatting | bytes 2097152 | tf_op jit(solution)/shard_map/reshape | solution.py:54
  9.6 7.4 %all-to-all-start = ((bf16[16,8,16,256]{3,2,0,1:T(8,128)(2,1)}), bf16[16,8,16,256]{3,2,0,1:T(8,128)(2,1)S(1)}, u32[]{:S(2)}, u32[]{:S(2)}) async-start(bf16[16,8,16,256]{3,2,0,1:T(8,128)(2,1)} %copy.23), calls=%async_computation | async-start | bytes 2097152 | tf_op jit(solution)/shard_map/all_to_all | solution.py:57
  17.1 25.6 %all-to-all-done = bf16[16,8,16,256]{3,2,0,1:T(8,128)(2,1)S(1)} async-done(((bf16[16,8,16,256]{3,2,0,1:T(8,128)(2,1)}), bf16[16,8,16,256]{3,2,0,1:T(8,128)(2,1)S(1)}, u32[]{:S(2)}, u32[]{:S(2)}) %all-to-all-start) | async-done | bytes 1048608 | tf_op jit(solution)/shard_map/all_to_all | solution.py:57
  42.8 0.3 convert_reduce_fusion
  43.1 0.7 fusion.43
  43.8 0.7 fusion.46
  44.6 0.3 copy.24
  44.9 0.5 fusion.79
  45.5 0.2 fusion.59
  45.8 10.6 %while.10 = (s32[]{:T(128)}, bf16[16,128,2,32]{1,3,2,0:T(8,128)(2,1)S(1)}, bf16[16,128,2,32]{1,3,2,0:T(8,128)(2,1)S(1)}, pred[128]{0:T(512)(128)(4,1)S(1)}, bf16...) while((s32[]{:T(128)}, ...), condition=%wide.region_5.6_spmd, body=%wide.region_2.5_spmd.sunk | while | flops 6537728 | bytes 137301 | solution.py:77
  45.8 0.3 fusion.98
  46.0 0.4 fusion.99
  46.4 0.3 fusion.98
  46.7 0.4 fusion.99
  47.1 0.3 fusion.98
  47.4 0.4 fusion.99
  47.8 0.3 fusion.98
  48.0 0.4 fusion.99
  48.4 0.3 fusion.98
  48.7 0.4 fusion.99
  49.1 0.3 fusion.98
  49.4 0.4 fusion.99
  49.7 0.3 fusion.98
  50.0 0.4 fusion.99
  50.4 0.3 fusion.98
  50.7 0.4 fusion.99
  51.1 0.3 fusion.98
  51.3 0.4 fusion.99
  51.7 0.3 fusion.98
  52.0 0.4 fusion.99
  52.4 0.3 fusion.98
  52.7 0.4 fusion.99
  53.1 0.3 fusion.98
  53.3 0.4 fusion.99
  53.7 0.3 fusion.98
  54.0 0.4 fusion.99
  54.4 0.3 fusion.98
  54.7 0.4 fusion.99
  55.0 0.3 fusion.98
  55.3 0.4 fusion.99
  55.7 0.3 fusion.98
  56.0 0.4 fusion.99
  56.4 0.9 copy.25
  57.3 0.5 dot_general.33
  57.9 1.4 convolution_convert_fusion
  59.4 0.6 fusion.78
  60.0 0.1 reshape.285
  61.1 33.8 %all-reduce.2.cloned.1.call-done = bf16[8,4,4,16,256]{4,3,2,1,0:T(8,128)(2,1)} async-done(((bf16[8,4,4,16,256]{4,3,2,1,0:T(8,128)(2,1)}), bf16[8,4,4,16,256]{4,3,2,1,0:T(8,128)(2,1)}) %all-reduce.2.cloned.1.call-update) | async-done | bytes 1048592 | tf_op jit(solution)/shard_map/psum | solution.py:91
  94.8 1.7 convert_reduce_fusion.1
  96.6 1.2 fusion.50
  97.9 1.2 fusion.53
  99.0 0.2 fusion.69
  99.2 0.2 fusion.67
  99.4 0.2 copy.33
  99.6 0.2 copy.34
  99.9 33.2 %all_gather.3 = bf16[32,128,32]{0,1,2:T(8,128)(2,1)S(1)} all-gather(bf16[32,16,32]{0,1,2:T(8,128)(2,1)S(1)} %get-tuple-element.61), channel_id=1, replica_groups=mesh['dap'=8,'head'=4] {'dap'}, dimensions={1}, use_global_device_ids=true | all-gather | bytes 294912 | tf_op jit(solution)/shard_map/all_gather | solution.py:130
  133.1 1.3 convolution_bitcast_fusion.1
  134.3 6.5 %copy.28 = f32[16,128,32,32]{1,3,2,0:T(8,128)S(1)} copy(f32[16,128,32,32]{1,2,3,0:T(8,128)S(1)} %convolution_bitcast_fusion.1) | data formatting | bytes 16777216 | tf_op jit(solution)/shard_map/transpose | solution.py:134
  140.8 14.9 %fusion.61 = f32[16,128,128]{2,1,0:T(8,128)} fusion(f32[16,128,1024]{1,2,0:T(8,128)S(1)} %bitcast.147, f32[1024,128]{1,0:T(8,128)S(1)} %copy-done), kind=kOutput, calls=%fused_computation.52 | convolution fusion | flops 3221225472 | bytes 9961472 | tf_op jit(solution)/shard_map/dot_general | solution.py:135
  155.7 5.4 %all-to-all-start.1 = ((bf16[32,16,256]{2,1,0:T(8,128)(2,1)}), bf16[32,16,256]{2,1,0:T(8,128)(2,1)S(1)}, u32[]{:S(2)}, u32[]{:S(2)}) async-start(bf16[32,16,256]{2,1,0:T(8,128)(2,1)} %bitcast.29), calls=%async_computation.1 | async-start | bytes 524288 | tf_op jit(solution)/shard_map/all_to_all | solution.py:95
  161.2 8.1 %all-to-all-done.1 = bf16[32,16,256]{2,1,0:T(8,128)(2,1)S(1)} async-done(((bf16[32,16,256]{2,1,0:T(8,128)(2,1)}), bf16[32,16,256]{2,1,0:T(8,128)(2,1)S(1)}, u32[]{:S(2)}, u32[]{:S(2)}) %all-to-all-start.1) | async-done | bytes 262176 | tf_op jit(solution)/shard_map/all_to_all | solution.py:95
  169.3 0.7 copy.26
  170.0 10.8 %reduce-scatter.2.cloned.1.call-done = f32[16,32,128]{2,1,0:T(8,128)} async-done(((f32[16,128,128]{2,1,0:T(8,128)}), f32[16,32,128]{2,1,0:T(8,128)}) %reduce-scatter.2.cloned.1.call-update) | async-done | bytes 262160 | tf_op jit(solution)/shard_map/reduce_scatter | solution.py:141
  180.8 1.8 add_divide_fusion
  (46 shorter events, 0.9 us)
Async XLA Ops:
  7.2 133.6 %copy-start = (f32[1024,128]{1,0:T(8,128)S(1)}, f32[1024,128]{1,0:T(8,128)}, u32[]{:S(2)}) copy-start(f32[1024,128]{1,0:T(8,128)} %param.28) | copy-start | bytes 1572868
  7.2 9.9 %copy-start.11 = (f32[64]{0:T(128)S(1)}, f32[64]{0:T(128)}, u32[]{:S(2)}) copy-start(f32[64]{0:T(128)} %param.22) | copy-start | bytes 772
  7.2 9.9 %copy-start.12 = (s32[128]{0:T(128)S(1)}, s32[128]{0:T(128)}, u32[]{:S(2)}) copy-start(s32[128]{0:T(128)} %param.17) | copy-start | bytes 1540
  9.6 34.2 %copy-start.4 = (f32[256]{0:T(256)S(1)}, f32[256]{0:T(256)}, u32[]{:S(2)}) copy-start(f32[256]{0:T(256)} %param.20) | copy-start | bytes 3076
  9.6 34.2 %copy-start.5 = (f32[256]{0:T(256)S(1)}, f32[256]{0:T(256)}, u32[]{:S(2)}) copy-start(f32[256]{0:T(256)} %param.19) | copy-start | bytes 3076
  9.6 33.2 %all-to-all-start = ((bf16[16,8,16,256]{3,2,0,1:T(8,128)(2,1)}), bf16[16,8,16,256]{3,2,0,1:T(8,128)(2,1)S(1)}, u32[]{:S(2)}, u32[]{:S(2)}) async-start(bf16[16,8,16,256]{3,2,0,1:T(8,128)(2,1)} %copy.23), calls=%async_computation | async-start | bytes 2097152 | tf_op jit(solution)/shard_map/all_to_all | solution.py:57
  17.0 77.9 %all-reduce.2.cloned.1.call-start = ((), (), s32[]{:S(2)}) async-start(), calls=%async_computation.3 | async-start | bytes 2097152 | tf_op jit(solution)/shard_map/psum | solution.py:91
  43.8 1.1 copy-start.1
  56.4 1.5 copy-start.2
  57.3 3.6 %copy-start.10 = (s32[128]{0:T(128)S(1)}, s32[128]{0:T(128)}, u32[]{:S(2)}) copy-start(s32[128]{0:T(128)} %param.18) | copy-start | bytes 1540
  57.3 37.5 %copy-start.6 = (f32[256]{0:T(256)S(1)}, f32[256]{0:T(256)}, u32[]{:S(2)}) copy-start(f32[256]{0:T(256)} %param.24) | copy-start | bytes 3076
  57.8 40.0 %copy-start.7 = (f32[256]{0:T(256)S(1)}, f32[256]{0:T(256)}, u32[]{:S(2)}) copy-start(f32[256]{0:T(256)} %param.26) | copy-start | bytes 3076
  57.9 40.0 %copy-start.8 = (f32[256]{0:T(256)S(1)}, f32[256]{0:T(256)}, u32[]{:S(2)}) copy-start(f32[256]{0:T(256)} %param.25) | copy-start | bytes 3076
  57.9 41.2 %copy-start.3 = (bf16[256,2,32]{0,2,1:T(8,128)(2,1)S(1)}, bf16[256,2,32]{0,2,1:T(8,128)(2,1)}, u32[]{:S(2)}) copy-start(bf16[256,2,32]{0,2,1:T(8,128)(2,1)} %param.27) | copy-start | bytes 98308
  59.3 121.5 %reduce-scatter.2.cloned.1.call-start = ((), (), s32[]{:S(2)}) async-start(), calls=%async_computation.4 | async-start | bytes 1310720 | tf_op jit(solution)/shard_map/reduce_scatter | solution.py:141
  155.7 25.1 %copy-start.9 = (f32[128]{0:T(128)S(1)}, f32[128]{0:T(128)}, u32[]{:S(2)}) copy-start(f32[128]{0:T(128)} %param.29) | copy-start | bytes 1540
  155.7 13.6 %all-to-all-start.1 = ((bf16[32,16,256]{2,1,0:T(8,128)(2,1)}), bf16[32,16,256]{2,1,0:T(8,128)(2,1)S(1)}, u32[]{:S(2)}, u32[]{:S(2)}) async-start(bf16[32,16,256]{2,1,0:T(8,128)(2,1)} %bitcast.29), calls=%async_computation.1 | async-start | bytes 524288 | tf_op jit(solution)/shard_map/all_to_all | solution.py:95
Sparse Core Ops, SparseCore 0:
  59.5 35.3 all-reduce.1
  155.9 24.9 reduce-scatter.1
where the time goes:
time: 190 us; the launch traced here: 189 us
  waiting for transfers between devices  78.3 us (41%)
  blocking collectives  33.2 us (17%)
  matrix products  29 us (15%)
  between operations  15.1 us (8%)
  starting transfers between devices  12.8 us (7%)
  local copies, waits for them, and re-layouts  12.1 us (6%)
  other arithmetic  8.95 us (5%)
    psum x1, waiting for transfers between devices, per_device(): lax.psum(partial_value.astype(jnp.bfloat16), 'head').astype(jnp.float32)  33.8 us
    all_gather x1, blocking collectives, per_device(): piece = lax.all_gather(right, 'dap', axis=1, tiled=True)  33.2 us
    all_to_all x1, waiting for transfers between devices, per_device(): lax.all_to_all(bundled_focus_units, 'dap', split_axis=1, concat_axis=0, t...  25.6 us
    dot_general x1, matrix products, per_device(): jnp.dot(outer, tensor_final_matrix, precision=lax.Precision.HIGHEST, pref...  14.9 us
    reduce_scatter x1, waiting for transfers between devices, per_device(): lax.psum_scatter(partial_pair, 'head', scatter_dimension=1, tiled=True)  10.8 us
    all_to_all x1, waiting for transfers between devices, per_device(): lax.all_to_all(mine.reshape(parallel_devices * group, residue_device_coun...  8.07 us
    all_to_all x1, starting transfers between devices, per_device(): lax.all_to_all(bundled_focus_units, 'dap', split_axis=1, concat_axis=0, t...  7.41 us
    transpose x1, local copies, waits for them, and re-layouts, per_device(): outer.transpose(0, 2, 1, 3)  6.49 us
  transfers between devices with their start and end apart: 4, of which 4 were waited for; matrix products, arithmetic and copies ran while one was open for 1% of the time, Pallas kernels for 0%

commit v1 on v0

--- a/solution.py
+++ b/solution.py
@@ -54,7 +54,12 @@
     bundled_focus_units = multiple_aligned_family.reshape(
         homolog_shard_number, parallel_devices, residue_device_count, feature_dimension
     )
-    received = lax.all_to_all(bundled_focus_units, "dap", split_axis=1, concat_axis=0, tiled=True)
+    received = jnp.concatenate(
+        lax.all_to_all(
+            jnp.stack(jnp.split(bundled_focus_units, lax.axis_size("dap"), axis=1)), "dap", 0, 0
+        ),
+        axis=0,
+    )
     block = received[:, 0]
     count = block.shape[1]
     normed = layer_norm(

time: 190 us -> 202 us (1.063)
  local copies, waits for them, and re-layouts: 12.1 us -> 24 us
    unnamed x26 -> x33, local copies, waits for them, and re-layouts: 0.07 us -> 11.1 us
    all_gather x0 -> x1, local copies, waits for them, and re-layouts: none -> 2.39 us  [per_device(): piece = lax.all_gather(right, 'dap', axis=1, tiled=True)]
    reshape x1 -> x0, local copies, waits for them, and re-layouts: 2.37 us -> none  [per_device(): multiple_aligned_family.reshape(homolog_shard_number, parallel_devices, r...]
where the time goes in v1:
time: 202 us
  waiting for transfers between devices  78.3 us (39%)
  blocking collectives  33.2 us (16%)
  matrix products  29.5 us (15%)
  local copies, waits for them, and re-layouts  24 us (12%)
  between operations  15 us (7%)
  starting transfers between devices  12.7 us (6%)
  other arithmetic  8.92 us (4%)
    psum x1, waiting for transfers between devices, per_device(): lax.psum(partial_value.astype(jnp.bfloat16), 'head').astype(jnp.float32)  33.7 us
    all_gather x1, blocking collectives, per_device(): piece = lax.all_gather(right, 'dap', axis=1, tiled=True)  33.2 us
    all_to_all x1, waiting for transfers between devices, per_device(): lax.all_to_all(jnp.stack(jnp.split(bundled_focus_units, lax.axis_size('da...  25.6 us
    dot_general x1, matrix products, per_device(): jnp.dot(outer, tensor_final_matrix, precision=lax.Precision.HIGHEST, pref...  14.9 us
    unnamed x33, local copies, waits for them, and re-layouts  11.1 us
    reduce_scatter x1, waiting for transfers between devices, per_device(): lax.psum_scatter(partial_pair, 'head', scatter_dimension=1, tiled=True)  10.8 us
    all_to_all x1, waiting for transfers between devices, per_device(): lax.all_to_all(mine.reshape(parallel_devices * group, residue_device_coun...  8.07 us
    all_to_all x1, starting transfers between devices, per_device(): lax.all_to_all(jnp.stack(jnp.split(bundled_focus_units, lax.axis_size('da...  7.41 us
  transfers between devices with their start and end apart: 4, of which 4 were waited for; matrix products, arithmetic and copies ran while one was open for 1% of the time, Pallas kernels for 0%

profile of v1, /device:TPU:0, one launch (start us, length us, event | category | flops | bytes accessed | tf_op | source)
XLA Modules:
  0.0 201.6 jit_solution(9448846714906942660)
XLA Ops:
  7.2 1.6 fusion.76
  8.8 1.6 fusion.75
  10.4 1.6 fusion.74
  11.9 1.6 fusion.73
  13.5 1.6 fusion.72
  15.1 1.6 fusion.71
  16.6 1.6 fusion.70
  18.2 1.6 fusion.69
  19.8 7.4 %all-to-all-start = ((bf16[8,16,1,16,256]{4,3,1,2,0:T(8,128)(2,1)}), bf16[8,16,1,16,256]{4,3,1,2,0:T(8,128)(2,1)S(1)}, u32[]{:S(2)}, u32[]{:S(2)}) async-start(bf16[8,16,1,16,256]{4,3,1,2,0:T(8,128)(2,1)} %fusion.69), calls=%async_computation | async-start | bytes 2097152 | tf_op jit(solution)/shard_map/all_to_all | solution.py:58
  27.3 25.6 %all-to-all-done = bf16[8,16,1,16,256]{4,3,1,2,0:T(8,128)(2,1)S(1)} async-done(((bf16[8,16,1,16,256]{4,3,1,2,0:T(8,128)(2,1)}), bf16[8,16,1,16,256]{4,3,1,2,0:T(8,128)(2,1)S(1)}, u32[]{:S(2)}, u32[]{:S(2)}) %all-to-all-start) | async-done | bytes 1048608 | tf_op jit(solution)/shard_map/all_to_all | solution.py:58
  53.0 0.3 convert_reduce_fusion
  53.3 0.7 fusion.43
  54.0 0.7 fusion.46
  54.8 0.9 fusion.89
  56.1 10.6 %while.10 = (s32[]{:T(128)}, bf16[16,128,2,32]{1,3,2,0:T(8,128)(2,1)S(1)}, bf16[16,128,2,32]{1,3,2,0:T(8,128)(2,1)S(1)}, pred[128]{0:T(512)(128)(4,1)S(1)}, bf16...) while((s32[]{:T(128)}, ...), condition=%wide.region_5.6_spmd, body=%wide.region_2.5_spmd.sunk | while | flops 6537728 | bytes 137301 | solution.py:82
  56.3 0.4 fusion.108
  56.7 0.3 fusion.107
  57.0 0.4 fusion.108
  57.4 0.3 fusion.107
  57.7 0.4 fusion.108
  58.1 0.3 fusion.107
  58.3 0.4 fusion.108
  58.7 0.3 fusion.107
  59.0 0.4 fusion.108
  59.4 0.3 fusion.107
  59.7 0.4 fusion.108
  60.0 0.3 fusion.107
  60.3 0.4 fusion.108
  60.7 0.3 fusion.107
  61.0 0.4 fusion.108
  61.4 0.3 fusion.107
  61.6 0.4 fusion.108
  62.0 0.3 fusion.107
  62.3 0.4 fusion.108
  62.7 0.3 fusion.107
  63.0 0.4 fusion.108
  63.4 0.3 fusion.107
  63.6 0.4 fusion.108
  64.0 0.3 fusion.107
  64.3 0.4 fusion.108
  64.7 0.3 fusion.107
  65.0 0.4 fusion.108
  65.3 0.3 fusion.107
  65.6 0.4 fusion.108
  66.0 0.3 fusion.107
  66.3 0.4 fusion.108
  66.7 0.9 copy.61
  67.6 0.5 dot_general.33
  68.2 1.4 convolution_convert_fusion
  69.7 0.6 fusion.88
  71.4 33.7 %all-reduce.2.cloned.1.call-done = bf16[8,4,4,16,256]{4,3,2,1,0:T(8,128)(2,1)} async-done(((bf16[8,4,4,16,256]{4,3,2,1,0:T(8,128)(2,1)}), bf16[8,4,4,16,256]{4,3,2,1,0:T(8,128)(2,1)}) %all-reduce.2.cloned.1.call-update) | async-done | bytes 1048592 | tf_op jit(solution)/shard_map/psum | solution.py:96
  105.1 1.7 convert_reduce_fusion.1
  106.9 1.2 fusion.55
  108.1 1.2 fusion.58
  109.7 33.2 %all_gather.3 = bf16[32,128,32]{2,1,0:T(8,128)(2,1)S(1)} all-gather(bf16[32,16,32]{2,1,0:T(8,128)(2,1)S(1)} %fusion.48), channel_id=1, replica_groups=mesh['dap'=8,'head'=4] {'dap'}, dimensions={1}, use_global_device_ids=true | all-gather | bytes 294912 | tf_op jit(solution)/shard_map/all_gather | solution.py:135
  142.9 2.4 %copy.64 = bf16[32,128,32]{0,1,2:T(8,128)(2,1)S(1)} copy(bf16[32,128,32]{2,1,0:T(8,128)(2,1)S(1)} %all_gather.3) | data formatting | bytes 524288 | tf_op jit(solution)/shard_map/all_gather | solution.py:135
  145.3 1.3 convolution_bitcast_fusion.1
  146.6 6.5 %copy.65 = f32[16,128,32,32]{1,3,2,0:T(8,128)S(1)} copy(f32[16,128,32,32]{1,2,3,0:T(8,128)S(1)} %convolution_bitcast_fusion.1) | data formatting | bytes 16777216 | tf_op jit(solution)/shard_map/transpose | solution.py:139
  153.1 14.9 %fusion.66 = f32[16,128,128]{2,1,0:T(8,128)} fusion(f32[16,128,1024]{1,2,0:T(8,128)S(1)} %bitcast.183, f32[1024,128]{1,0:T(8,128)S(1)} %copy-done), kind=kOutput, calls=%fused_computation.59 | convolution fusion | flops 3221225472 | bytes 9961472 | tf_op jit(solution)/shard_map/dot_general | solution.py:140
  168.0 5.2 %all-to-all-start.1 = ((bf16[32,16,256]{2,1,0:T(8,128)(2,1)}), bf16[32,16,256]{2,1,0:T(8,128)(2,1)S(1)}, u32[]{:S(2)}, u32[]{:S(2)}) async-start(bf16[32,16,256]{2,1,0:T(8,128)(2,1)} %bitcast.33), calls=%async_computation.1 | async-start | bytes 524288 | tf_op jit(solution)/shard_map/all_to_all | solution.py:100
  173.3 8.1 %all-to-all-done.1 = bf16[32,16,256]{2,1,0:T(8,128)(2,1)S(1)} async-done(((bf16[32,16,256]{2,1,0:T(8,128)(2,1)}), bf16[32,16,256]{2,1,0:T(8,128)(2,1)S(1)}, u32[]{:S(2)}, u32[]{:S(2)}) %all-to-all-start.1) | async-done | bytes 262176 | tf_op jit(solution)/shard_map/all_to_all | solution.py:100
  181.4 0.7 copy.62
  182.1 10.8 %reduce-scatter.2.cloned.1.call-done = f32[16,32,128]{2,1,0:T(8,128)} async-done(((f32[16,128,128]{2,1,0:T(8,128)}), f32[16,32,128]{2,1,0:T(8,128)}) %reduce-scatter.2.cloned.1.call-update) | async-done | bytes 262160 | tf_op jit(solution)/shard_map/reduce_scatter | solution.py:146
  192.9 1.8 add_divide_fusion
  (50 shorter events, 1.8 us)
Async XLA Ops:
  7.2 145.9 %copy-start = (f32[1024,128]{1,0:T(8,128)S(1)}, f32[1024,128]{1,0:T(8,128)}, u32[]{:S(2)}) copy-start(f32[1024,128]{1,0:T(8,128)} %param.28) | copy-start | bytes 1572868
  7.2 20.1 %copy-start.11 = (f32[64]{0:T(128)S(1)}, f32[64]{0:T(128)}, u32[]{:S(2)}) copy-start(f32[64]{0:T(128)} %param.22) | copy-start | bytes 772
  7.2 20.1 %copy-start.12 = (s32[128]{0:T(128)S(1)}, s32[128]{0:T(128)}, u32[]{:S(2)}) copy-start(s32[128]{0:T(128)} %param.17) | copy-start | bytes 1540
  19.8 34.3 %copy-start.4 = (f32[256]{0:T(256)S(1)}, f32[256]{0:T(256)}, u32[]{:S(2)}) copy-start(f32[256]{0:T(256)} %param.20) | copy-start | bytes 3076
  19.8 34.3 %copy-start.5 = (f32[256]{0:T(256)S(1)}, f32[256]{0:T(256)}, u32[]{:S(2)}) copy-start(f32[256]{0:T(256)} %param.19) | copy-start | bytes 3076
  19.8 33.2 %all-to-all-start = ((bf16[8,16,1,16,256]{4,3,1,2,0:T(8,128)(2,1)}), bf16[8,16,1,16,256]{4,3,1,2,0:T(8,128)(2,1)S(1)}, u32[]{:S(2)}, u32[]{:S(2)}) async-start(bf16[8,16,1,16,256]{4,3,1,2,0:T(8,128)(2,1)} %fusion.69), calls=%async_computation | async-start | bytes 2097152 | tf_op jit(solution)/shard_map/all_to_all | solution.py:58
  27.2 77.9 %all-reduce.2.cloned.1.call-start = ((), (), s32[]{:S(2)}) async-start(), calls=%async_computation.3 | async-start | bytes 2097152 | tf_op jit(solution)/shard_map/psum | solution.py:96
  53.3 1.5 copy-start.1
  66.7 1.5 copy-start.2
  67.6 3.6 %copy-start.10 = (s32[128]{0:T(128)S(1)}, s32[128]{0:T(128)}, u32[]{:S(2)}) copy-start(s32[128]{0:T(128)} %param.18) | copy-start | bytes 1540
  67.6 37.5 %copy-start.6 = (f32[256]{0:T(256)S(1)}, f32[256]{0:T(256)}, u32[]{:S(2)}) copy-start(f32[256]{0:T(256)} %param.24) | copy-start | bytes 3076
  68.1 40.0 %copy-start.7 = (f32[256]{0:T(256)S(1)}, f32[256]{0:T(256)}, u32[]{:S(2)}) copy-start(f32[256]{0:T(256)} %param.26) | copy-start | bytes 3076
  68.2 40.0 %copy-start.8 = (f32[256]{0:T(256)S(1)}, f32[256]{0:T(256)}, u32[]{:S(2)}) copy-start(f32[256]{0:T(256)} %param.25) | copy-start | bytes 3076
  68.2 41.1 %copy-start.3 = (bf16[256,2,32]{0,2,1:T(8,128)(2,1)S(1)}, bf16[256,2,32]{0,2,1:T(8,128)(2,1)}, u32[]{:S(2)}) copy-start(bf16[256,2,32]{0,2,1:T(8,128)(2,1)} %param.27) | copy-start | bytes 98308
  69.6 123.3 %reduce-scatter.2.cloned.1.call-start = ((), (), s32[]{:S(2)}) async-start(), calls=%async_computation.4 | async-start | bytes 1310720 | tf_op jit(solution)/shard_map/reduce_scatter | solution.py:146
  168.0 25.0 %copy-start.9 = (f32[128]{0:T(128)S(1)}, f32[128]{0:T(128)}, u32[]{:S(2)}) copy-start(f32[128]{0:T(128)} %param.29) | copy-start | bytes 1540
  168.0 13.4 %all-to-all-start.1 = ((bf16[32,16,256]{2,1,0:T(8,128)(2,1)}), bf16[32,16,256]{2,1,0:T(8,128)(2,1)S(1)}, u32[]{:S(2)}, u32[]{:S(2)}) async-start(bf16[32,16,256]{2,1,0:T(8,128)(2,1)} %bitcast.33), calls=%async_computation.1 | async-start | bytes 524288 | tf_op jit(solution)/shard_map/all_to_all | solution.py:100
Sparse Core Ops, SparseCore 0:
  69.8 35.2 all-reduce.1
  168.1 24.7 reduce-scatter.1
